TPU v7x, 128 devices: a whole 4x4x4 slice. The times are simulated.
128 devices in a mesh: rows: 4 (over x), cols: 32 (over y, z, core).
Axes of the slice: x: 4, y: 4, z: 4, core: 2. Of those that a mesh axis runs over, the one named last changes fastest.
Arguments:
- left_image: bfloat16 [128, 8192], P(('rows', 'cols')), may hold values from -8 to 8, as said below
- right_image: bfloat16 [128, 8192], P(('rows', 'cols')), may hold values from -8 to 8, as said below
- ranges: int32 [32, 2], replicated, may hold values from 0 to 63, as said below
Outputs:
- best_score: float32 [128, 8192], P('rows', 'cols')
Inputs may be any that keep to these rules, and one draw needn't show every extreme that they name: `left_image`: pixel values. `right_image`: pixel values. `ranges`: row t holds tile t's first disparity (column 0, 0 to 63) and its number of blocks of 128 disparities (column 1, 1 to 2); some tile has 2 blocks, some tile starts at 0 and some at 63.
All inputs are finite; a program needn't handle non-finite values.
Results may differ from a plain program's by a relative error of at most 0.0003.
Values may be sent and summed in bfloat16 or wider, within the bound.
A program may use at most 128 MiB of HBM per device.

v0:
```python
import jax
import jax.numpy as jnp
from jax import lax
from jax.experimental import pallas as pl
from jax.experimental.pallas import tpu as pltpu
from jax.sharding import PartitionSpec as P

F32, BF16 = jnp.float32, jnp.bfloat16

def split3(x):
    hi = x.astype(BF16)
    r = x - hi.astype(F32)
    mid = r.astype(BF16)
    lo = (r - mid.astype(F32)).astype(BF16)
    return hi, mid, lo

def box_rows(h):
    out = h[0:32]
    for i in range(1, 7):
        out = out + h[i:i + 32]
    return out

def stats(shifted):
    h = shifted[0]
    q = shifted[0] * shifted[0]
    for v in shifted[1:]:
        h = h + v
        q = q + v * v
    total = box_rows(h)
    mean = total * (1.0 / 49.0)
    spread = jnp.maximum(box_rows(q) * (1.0 / 49.0) - mean * mean, 0.01)
    return total, mean, lax.rsqrt(spread)

def compute(L, R, s, two, out_ref, acc_ref):
    Ls = pltpu.roll(L, 768 - 381, 1)
    Lj = [Ls[:, :256]] + [pltpu.roll(Ls, 768 - j, 1)[:, :256] for j in range(1, 7)]
    Rs = pltpu.roll(R, 642 + s, 1)[:, :640]
    Rj = [Rs[:, :512]] + [pltpu.roll(Rs, 640 - j, 1)[:, :512] for j in range(1, 7)]
    SL, _, IL = stats(Lj)
    _, MR, IR = stats(Rj)
    a = split3(-SL)
    b = split3(MR)
    pairs = ((0, 0), (0, 1), (1, 0), (1, 1), (0, 2), (2, 0))
    m = lax.broadcasted_iota(jnp.int32, (128, 128), 1) >= lax.broadcasted_iota(jnp.int32, (128, 128), 0)
    lane = lax.broadcasted_iota(jnp.int32, (1, 160), 1)
    place = jnp.where(lane < 112, lane % 16, (lane - 112) % 8)
    width = jnp.where(lane < 112, 6, 0)
    for blk in range(4):
        y0 = 8 * blk
        rt = jnp.concatenate([v[y0:y0 + 16].astype(BF16) for v in Rj]
                             + [jnp.concatenate([b[q][y0:y0 + 8].astype(F32) for _, q in pairs], 0).astype(BF16)], 0)
        lt = jnp.concatenate([v[y0:y0 + 16] for v in Lj]
                             + [a[p][y0:y0 + 8].astype(F32) for p, _ in pairs], 0)
        lc = lt.T.astype(BF16)
        for yy in range(8):
            y = y0 + yy
            keep = (place >= yy) & (place <= yy + width)
            lhs = lc * keep.astype(F32).astype(BF16)
            g = jnp.dot(lhs, rt, preferred_element_type=F32)
            for X in range(2):
                rows = slice(128 * X, 128 * X + 128)
                gi = [g[rows, 128 * (X + k):128 * (X + k + 1)] * IR[y:y + 1, 128 * (X + k):128 * (X + k + 1)]
                      for k in range(3)]
                one = jnp.where(m, gi[1], gi[2])
                more = jnp.where(m, gi[0], gi[1])
                v = jnp.where(two, jnp.maximum(one, more), one)
                acc_ref[rows, y:y + 1] = jnp.max(v, axis=1, keepdims=True)
    best = acc_ref[...].T[:32] * IL * (1.0 / 49.0)
    out_ref[...] = jnp.maximum(best, -2.0)


EXTRA = 384
SPAN = 768
MESH = pl.DeviceIdType.MESH


def exchange(l_ref, r_ref, out_ref, stage, own_sem, send_sem, recv_sem):
    band, tile = lax.axis_index("rows"), lax.axis_index("cols")
    bands, tiles = lax.axis_size("rows"), lax.axis_size("cols")
    above, below = lax.rem(band + bands - 1, bands), lax.rem(band + 1, bands)
    edge_up, edge_down = tile < 3, tile >= tiles - 3
    width = l_ref.shape[1]

    barrier = pltpu.get_barrier_semaphore()

    def greet(other_band, other_tile):
        pl.semaphore_signal(barrier, inc=1, device_id=(other_band, other_tile), device_id_type=MESH)

    @pl.loop(1, tiles)
    def _(k):
        greet(band, lax.rem(tile + k, tiles))

    for k in range(3):
        greet(above, tiles - 3 + k)
        greet(below, k)

    stage[:, :EXTRA] = jnp.zeros((2, EXTRA), stage.dtype)
    stage[:, EXTRA + width:] = jnp.zeros((2, EXTRA), stage.dtype)
    stage[0:1, EXTRA:EXTRA + width] = l_ref[...]
    stage[1:2, EXTRA:EXTRA + width] = r_ref[...]

    def window(other):
        return stage.at[:, pl.ds(pl.multiple_of(other * 256, 256), SPAN)]

    def send(other_band, other_tile, row, slot):
        pltpu.make_async_remote_copy(
            src_ref=window(other_tile), dst_ref=out_ref.at[row], send_sem=send_sem.at[slot], recv_sem=recv_sem,
            device_id=(other_band, other_tile), device_id_type=MESH).start()

    own = pltpu.make_async_copy(window(tile), out_ref.at[tile + 3], own_sem)
    own.start()

    on_edge = edge_up | edge_down
    pl.semaphore_wait(barrier, tiles - 1 + jnp.where(on_edge, tiles, 0))

    @pl.when(edge_up)
    def _():
        @pl.loop(0, tiles)
        def _(k):
            send(above, lax.rem(tile + k, tiles), tiles + 3 + tile, 1)

    @pl.when(edge_down)
    def _():
        @pl.loop(0, tiles)
        def _(k):
            send(below, lax.rem(tile + k, tiles), tile - (tiles - 3), 1)

    @pl.loop(1, tiles)
    def _(k):
        send(band, lax.rem(tile + k, tiles), tile + 3, 0)

    own.wait()

    def bytes_of(count, sem):
        return pltpu.make_async_copy(out_ref.at[pl.ds(0, count)], out_ref.at[pl.ds(0, count)], sem)

    bytes_of(tiles + 5, recv_sem).wait()
    bytes_of(tiles - 1, send_sem.at[0]).wait()

    @pl.when(on_edge)
    def _():
        bytes_of(tiles, send_sem.at[1]).wait()


def scores(rng_ref, w_ref, out_ref, acc_ref):
    band, tile = lax.axis_index("rows"), lax.axis_index("cols")
    line = lax.broadcasted_iota(jnp.int32, (40, SPAN), 0) + (32 * band - 3)
    inside = (line >= 0) & (line < 32 * lax.axis_size("rows")) & (line < 32 * band + 35)
    w = w_ref[...].astype(F32)
    left = jnp.where(inside, w[:, 0, :], 0.0)
    right = jnp.where(inside, w[:, 1, :], 0.0)
    compute(left, right, rng_ref[tile, 0], rng_ref[tile, 1] > 1, out_ref, acc_ref)


def solution(mesh):
    VMEM = pl.BlockSpec(memory_space=pltpu.VMEM)

    def on_device(left_image, right_image, ranges):
        windows = pl.pallas_call(
            exchange,
            out_shape=jax.ShapeDtypeStruct((40, 2, SPAN), BF16),
            in_specs=[VMEM, VMEM],
            out_specs=VMEM,
            scratch_shapes=[
                pltpu.VMEM((2, left_image.shape[1] + 2 * EXTRA), BF16),
                pltpu.SemaphoreType.DMA,
                pltpu.SemaphoreType.DMA((2,)),
                pltpu.SemaphoreType.DMA,
            ],
            name="exchange",
            compiler_params=pltpu.CompilerParams(collective_id=0, has_side_effects=True),
        )(left_image, right_image)
        return pl.pallas_call(
            scores,
            out_shape=jax.ShapeDtypeStruct((32, 256), F32),
            in_specs=[pl.BlockSpec(memory_space=pltpu.SMEM), VMEM],
            out_specs=VMEM,
            scratch_shapes=[pltpu.VMEM((256, 128), F32)],
            name="scores",
            compiler_params=pltpu.CompilerParams(vmem_limit_bytes=48 << 20),
        )(ranges, windows)

    return jax.shard_map(
        on_device,
        mesh=mesh,
        in_specs=(P(("rows", "cols"), None), P(("rows", "cols"), None), P()),
        out_specs=P("rows", "cols"),
        check_vma=False,
    )
```

profile of v0, /device:TPU:1, one launch (start us, length us, event | category | flops | bytes accessed | tf_op | source)
XLA Modules:
  0.0 20.8 jit_solution(8505762907275124988)
XLA Ops:
  0.0 0.8 %copy.4.rng_ref = s32[32,2]{1,0:T(8,128)S(1)} copy(s32[32,2]{0,1:T(2,128)} %param.5) | data formatting | bytes 512 | tf_op args[2]
  0.8 14.7 %exchange.1.w_ref = bf16[40,2,768]{2,1,0:T(2,128)(2,1)} custom-call(bf16[1,8192]{1,0:T(2,128)(2,1)} %l_ref.1, bf16[1,8192]{1,0:T(2,128)(2,1)} %r_ref.1), custom_call_target="tpu_custom_call" | custom-call | tf_op jit(solution)/shard_map/exchange/pallas_call | solution.py:159
  15.5 0.0 copy-start
  15.5 0.9 %copy-done = bf16[40,2,768]{2,1,0:T(2,128)(2,1)S(1)} copy-done((bf16[40,2,768]{2,1,0:T(2,128)(2,1)S(1)}, bf16[40,2,768]{2,1,0:T(2,128)(2,1)}, u32[]{:S(2)}) %copy-start) | copy-done | bytes 122904
  16.4 4.4 %scores.1 = f32[32,256]{1,0:T(8,128)} custom-call(s32[32,2]{1,0:T(8,128)S(1)} %copy.4.rng_ref, bf16[40,2,768]{2,1,0:T(2,128)(2,1)S(1)} %copy-done), custom_call_target="tpu_custom_call" | custom-call | tf_op jit(solution)/shard_map/scores/pallas_call | solution.py:173
Async XLA Ops:
  15.5 0.9 %copy-start = (bf16[40,2,768]{2,1,0:T(2,128)(2,1)S(1)}, bf16[40,2,768]{2,1,0:T(2,128)(2,1)}, u32[]{:S(2)}) copy-start(bf16[40,2,768]{2,1,0:T(2,128)(2,1)} %exchange.1.w_ref) | copy-start | bytes 368644
where the time goes:
time: 21 us; the launch traced here: 20.8 us
  Pallas kernels  19.1 us (91%)
  local copies, waits for them, and re-layouts  1.65 us (8%)
    pallas_call x1, Pallas kernels, on_device(): pl.pallas_call(exchange, out_shape=jax.ShapeDtypeStruct((40, 2, SPAN), BF...  14.7 us
    pallas_call x1, Pallas kernels, on_device(): pl.pallas_call(scores, out_shape=jax.ShapeDtypeStruct((32, 256), F32), in...  4.43 us
    unnamed x3, local copies, waits for them, and re-layouts  1.65 us

commit v1 on v0

--- a/solution.py
+++ b/solution.py
@@ -69,77 +69,98 @@
     out_ref[...] = jnp.maximum(best, -2.0)
 
 
-EXTRA = 384
 SPAN = 768
+PAD = 384
 MESH = pl.DeviceIdType.MESH
-
-
-def exchange(l_ref, r_ref, out_ref, stage, own_sem, send_sem, recv_sem):
+OFFSETS = sorted(((dy, dz) for dy in range(4) for dz in range(4)), key=lambda o: -(2 - abs(o[0] - 2)) - (2 - abs(o[1] - 2)))
+
+
+def exchange(l_hbm, r_hbm, out_ref, l_row, r_row, stage, load_sem, own_sem, send_sem, recv_sem):
     band, tile = lax.axis_index("rows"), lax.axis_index("cols")
     bands, tiles = lax.axis_size("rows"), lax.axis_size("cols")
-    above, below = lax.rem(band + bands - 1, bands), lax.rem(band + 1, bands)
-    edge_up, edge_down = tile < 3, tile >= tiles - 3
-    width = l_ref.shape[1]
-
+    width = l_hbm.shape[1]
+    y, z, core = tile // 8, tile // 2 % 4, tile % 2
+    goes_up = (tile < 3) & (band > 0)
+    goes_down = (tile >= tiles - 3) & (band < bands - 1)
+    other = jnp.where(goes_up, band - 1, band + 1)
+    crosses = goes_up | goes_down
     barrier = pltpu.get_barrier_semaphore()
+
+    loads = [pltpu.make_async_copy(l_hbm, l_row, load_sem.at[0]), pltpu.make_async_copy(r_hbm, r_row, load_sem.at[1])]
+    for load in loads:
+        load.start()
 
     def greet(other_band, other_tile):
         pl.semaphore_signal(barrier, inc=1, device_id=(other_band, other_tile), device_id_type=MESH)
 
-    @pl.loop(1, tiles)
-    def _(k):
-        greet(band, lax.rem(tile + k, tiles))
-
-    for k in range(3):
-        greet(above, tiles - 3 + k)
-        greet(below, k)
-
-    stage[:, :EXTRA] = jnp.zeros((2, EXTRA), stage.dtype)
-    stage[:, EXTRA + width:] = jnp.zeros((2, EXTRA), stage.dtype)
-    stage[0:1, EXTRA:EXTRA + width] = l_ref[...]
-    stage[1:2, EXTRA:EXTRA + width] = r_ref[...]
-
-    def window(other):
-        return stage.at[:, pl.ds(pl.multiple_of(other * 256, 256), SPAN)]
-
-    def send(other_band, other_tile, row, slot):
+    def peers(dy, dz):
+        chip = (y + dy) % 4 * 8 + (z + dz) % 4 * 2
+        return [chip + 1 - core] + ([chip + core] if dy or dz else [])
+
+    @pl.when(band > 0)
+    def _():
+        for k in range(3):
+            greet(band - 1, tiles - 3 + k)
+
+    @pl.when(band < bands - 1)
+    def _():
+        for k in range(3):
+            greet(band + 1, k)
+
+    for dy, dz in OFFSETS:
+        for peer in peers(dy, dz):
+            greet(band, peer)
+
+    for load in loads:
+        load.wait()
+    stage[:, :PAD] = jnp.zeros((2, PAD), stage.dtype)
+    stage[:, PAD + width:] = jnp.zeros((2, PAD), stage.dtype)
+    stage[0:1, PAD:PAD + width] = l_row[...]
+    stage[1:2, PAD:PAD + width] = r_row[...]
+
+    def window(peer):
+        return stage.at[:, pl.ds(pl.multiple_of(peer * 256, 256), SPAN)]
+
+    def send(other_band, peer, row, slot, kind):
         pltpu.make_async_remote_copy(
-            src_ref=window(other_tile), dst_ref=out_ref.at[row], send_sem=send_sem.at[slot], recv_sem=recv_sem,
-            device_id=(other_band, other_tile), device_id_type=MESH).start()
+            src_ref=window(peer), dst_ref=out_ref.at[row], send_sem=send_sem.at[slot], recv_sem=recv_sem.at[kind],
+            device_id=(other_band, peer), device_id_type=MESH).start()
 
     own = pltpu.make_async_copy(window(tile), out_ref.at[tile + 3], own_sem)
     own.start()
-
-    on_edge = edge_up | edge_down
-    pl.semaphore_wait(barrier, tiles - 1 + jnp.where(on_edge, tiles, 0))
-
-    @pl.when(edge_up)
-    def _():
-        @pl.loop(0, tiles)
-        def _(k):
-            send(above, lax.rem(tile + k, tiles), tiles + 3 + tile, 1)
-
-    @pl.when(edge_down)
-    def _():
-        @pl.loop(0, tiles)
-        def _(k):
-            send(below, lax.rem(tile + k, tiles), tile - (tiles - 3), 1)
-
-    @pl.loop(1, tiles)
-    def _(k):
-        send(band, lax.rem(tile + k, tiles), tile + 3, 0)
+    pl.semaphore_wait(barrier, tiles - 1 + jnp.where(crosses, tiles, 0))
+    row_there = jnp.where(goes_up, tiles + 3 + tile, tile - (tiles - 3))
+    kind_there = jnp.where(goes_up, 2, 1)
+    for dy, dz in OFFSETS:
+        for peer in peers(dy, dz):
+            send(band, peer, tile + 3, 0, 0)
+
+        @pl.when(crosses)
+        def _():
+            chip = (y + dy) % 4 * 8 + (z + dz) % 4 * 2
+            send(other, chip, row_there, 1, kind_there)
+            send(other, chip + 1, row_there, 1, kind_there)
+
+    def wait_for(count, sem):
+        rows = out_ref.at[pl.ds(0, count)]
+        pltpu.make_async_copy(rows, rows, sem).wait()
 
     own.wait()
-
-    def bytes_of(count, sem):
-        return pltpu.make_async_copy(out_ref.at[pl.ds(0, count)], out_ref.at[pl.ds(0, count)], sem)
-
-    bytes_of(tiles + 5, recv_sem).wait()
-    bytes_of(tiles - 1, send_sem.at[0]).wait()
-
-    @pl.when(on_edge)
-    def _():
-        bytes_of(tiles, send_sem.at[1]).wait()
+    wait_for(tiles - 1, recv_sem.at[0])
+
+    @pl.when(band > 0)
+    def _():
+        wait_for(3, recv_sem.at[1])
+
+    @pl.when(band < bands - 1)
+    def _():
+        wait_for(3, recv_sem.at[2])
+
+    wait_for(tiles - 1, send_sem.at[0])
+
+    @pl.when(crosses)
+    def _():
+        wait_for(tiles, send_sem.at[1])
 
 
 def scores(rng_ref, w_ref, out_ref, acc_ref):
@@ -149,7 +170,7 @@
     w = w_ref[...].astype(F32)
     left = jnp.where(inside, w[:, 0, :], 0.0)
     right = jnp.where(inside, w[:, 1, :], 0.0)
-    compute(left, right, rng_ref[tile, 0], rng_ref[tile, 1] > 1, out_ref, acc_ref)
+    compute(left, right, rng_ref[0, tile], rng_ref[1, tile] > 1, out_ref, acc_ref)
 
 
 def solution(mesh):
@@ -159,17 +180,20 @@
         windows = pl.pallas_call(
             exchange,
             out_shape=jax.ShapeDtypeStruct((40, 2, SPAN), BF16),
-            in_specs=[VMEM, VMEM],
+            in_specs=[pl.BlockSpec(memory_space=pltpu.HBM)] * 2,
             out_specs=VMEM,
             scratch_shapes=[
-                pltpu.VMEM((2, left_image.shape[1] + 2 * EXTRA), BF16),
+                pltpu.VMEM(left_image.shape, BF16),
+                pltpu.VMEM(right_image.shape, BF16),
+                pltpu.VMEM((2, left_image.shape[1] + 2 * PAD), BF16),
+                pltpu.SemaphoreType.DMA((2,)),
                 pltpu.SemaphoreType.DMA,
                 pltpu.SemaphoreType.DMA((2,)),
-                pltpu.SemaphoreType.DMA,
+                pltpu.SemaphoreType.DMA((3,)),
             ],
             name="exchange",
-            compiler_params=pltpu.CompilerParams(collective_id=0, has_side_effects=True),
-        )(left_image, right_image)
+            compiler_params=pltpu.CompilerParams(collective_id=0, has_side_effects=True, vmem_limit_bytes=4 << 20),
+        )(*(pltpu.with_memory_space_constraint(x, pltpu.HBM) for x in (left_image, right_image)))
         return pl.pallas_call(
             scores,
             out_shape=jax.ShapeDtypeStruct((32, 256), F32),
@@ -177,8 +201,8 @@
             out_specs=VMEM,
             scratch_shapes=[pltpu.VMEM((256, 128), F32)],
             name="scores",
-            compiler_params=pltpu.CompilerParams(vmem_limit_bytes=48 << 20),
-        )(ranges, windows)
+            compiler_params=pltpu.CompilerParams(vmem_limit_bytes=12 << 20),
+        )(ranges.T, windows)
 
     return jax.shard_map(
         on_device,

time: 21 us -> 16.8 us (0.80)
  Pallas kernels: 19.1 us -> 16.6 us
  local copies, waits for them, and re-layouts: 1.65 us -> 0.01 us
    pallas_call x1, Pallas kernels: 14.7 us -> 12.5 us  [on_device(): pl.pallas_call(exchange, out_shape=jax.ShapeDtypeStruct((40, 2, SPAN), BF...]
    unnamed x3 -> x2, local copies, waits for them, and re-layouts: 1.65 us -> 0.01 us
    pallas_call x1, Pallas kernels: 4.43 us -> 4.18 us  [on_device(): pl.pallas_call(scores, out_shape=jax.ShapeDtypeStruct((32, 256), F32), in...]
where the time goes in v1:
time: 16.8 us; the launch traced here: 16.6 us
  Pallas kernels  16.6 us (99%)
    pallas_call x1, Pallas kernels, on_device(): pl.pallas_call(exchange, out_shape=jax.ShapeDtypeStruct((40, 2, SPAN), BF...  12.5 us
    pallas_call x1, Pallas kernels, on_device(): pl.pallas_call(scores, out_shape=jax.ShapeDtypeStruct((32, 256), F32), in...  4.18 us

profile of v1, /device:TPU:1, one launch (start us, length us, event | category | flops | bytes accessed | tf_op | source)
XLA Modules:
  0.0 16.6 jit_solution(16537345808189427720)
XLA Ops:
  0.0 0.0 copy-start
  0.0 12.5 %exchange.1.w_ref = bf16[40,2,768]{2,1,0:T(2,128)(2,1)S(1)} custom-call(bf16[1,8192]{1,0:T(2,128)(2,1)} %l_hbm.1, bf16[1,8192]{1,0:T(2,128)(2,1)} %r_hbm.1), custom_call_target="tpu_custom_call" | custom-call | tf_op jit(solution)/shard_map/exchange/pallas_call | solution.py:180
  12.5 0.0 copy-done
  12.5 4.2 %scores.1 = f32[32,256]{1,0:T(8,128)} custom-call(s32[2,32]{1,0:T(2,128)S(1)} %bitcast.1, bf16[40,2,768]{2,1,0:T(2,128)(2,1)S(1)} %exchange.1.w_ref), custom_call_target="tpu_custom_call" | custom-call | tf_op jit(solution)/shard_map/scores/pallas_call | solution.py:197
Async XLA Ops:
  0.0 12.5 %copy-start = (s32[32,2]{0,1:T(2,128)S(1)}, s32[32,2]{0,1:T(2,128)}, u32[]{:S(2)}) copy-start(s32[32,2]{0,1:T(2,128)} %param.5) | copy-start | bytes 772

commit v2 on v1

--- a/solution.py
+++ b/solution.py
@@ -66,7 +66,7 @@
                 v = jnp.where(two, jnp.maximum(one, more), one)
                 acc_ref[rows, y:y + 1] = jnp.max(v, axis=1, keepdims=True)
     best = acc_ref[...].T[:32] * IL * (1.0 / 49.0)
-    out_ref[...] = jnp.maximum(best, -2.0)
+    out_ref[...] = best
 
 
 SPAN = 768
@@ -75,7 +75,7 @@
 OFFSETS = sorted(((dy, dz) for dy in range(4) for dz in range(4)), key=lambda o: -(2 - abs(o[0] - 2)) - (2 - abs(o[1] - 2)))
 
 
-def exchange(l_hbm, r_hbm, out_ref, l_row, r_row, stage, load_sem, own_sem, send_sem, recv_sem):
+def fused(rng_ref, l_hbm, r_hbm, best_ref, l_row, r_row, stage, out_ref, acc_ref, load_sem, own_sem, send_sem, recv_sem):
     band, tile = lax.axis_index("rows"), lax.axis_index("cols")
     bands, tiles = lax.axis_size("rows"), lax.axis_size("cols")
     width = l_hbm.shape[1]
@@ -156,53 +156,44 @@
     def _():
         wait_for(3, recv_sem.at[2])
 
-    wait_for(tiles - 1, send_sem.at[0])
-
-    @pl.when(crosses)
-    def _():
-        wait_for(tiles, send_sem.at[1])
-
-
-def scores(rng_ref, w_ref, out_ref, acc_ref):
-    band, tile = lax.axis_index("rows"), lax.axis_index("cols")
     line = lax.broadcasted_iota(jnp.int32, (40, SPAN), 0) + (32 * band - 3)
-    inside = (line >= 0) & (line < 32 * lax.axis_size("rows")) & (line < 32 * band + 35)
-    w = w_ref[...].astype(F32)
+    inside = (line >= 0) & (line < 32 * bands) & (line < 32 * band + 35)
+    w = out_ref[...].astype(F32)
     left = jnp.where(inside, w[:, 0, :], 0.0)
     right = jnp.where(inside, w[:, 1, :], 0.0)
-    compute(left, right, rng_ref[0, tile], rng_ref[1, tile] > 1, out_ref, acc_ref)
+    compute(left, right, rng_ref[0, tile], rng_ref[1, tile] > 1, best_ref, acc_ref)
+    wait_for(tiles - 1, send_sem.at[0])
+
+    @pl.when(crosses)
+    def _():
+        wait_for(tiles, send_sem.at[1])
 
 
 def solution(mesh):
     VMEM = pl.BlockSpec(memory_space=pltpu.VMEM)
 
     def on_device(left_image, right_image, ranges):
-        windows = pl.pallas_call(
-            exchange,
-            out_shape=jax.ShapeDtypeStruct((40, 2, SPAN), BF16),
-            in_specs=[pl.BlockSpec(memory_space=pltpu.HBM)] * 2,
+        images = [pltpu.with_memory_space_constraint(x, pltpu.HBM) for x in (left_image, right_image)]
+        best = pl.pallas_call(
+            fused,
+            out_shape=jax.ShapeDtypeStruct((32, 256), F32),
+            in_specs=[pl.BlockSpec(memory_space=pltpu.SMEM)] + [pl.BlockSpec(memory_space=pltpu.HBM)] * 2,
             out_specs=VMEM,
             scratch_shapes=[
                 pltpu.VMEM(left_image.shape, BF16),
                 pltpu.VMEM(right_image.shape, BF16),
                 pltpu.VMEM((2, left_image.shape[1] + 2 * PAD), BF16),
+                pltpu.VMEM((40, 2, SPAN), BF16),
+                pltpu.VMEM((256, 128), F32),
                 pltpu.SemaphoreType.DMA((2,)),
                 pltpu.SemaphoreType.DMA,
                 pltpu.SemaphoreType.DMA((2,)),
                 pltpu.SemaphoreType.DMA((3,)),
             ],
             name="exchange",
-            compiler_params=pltpu.CompilerParams(collective_id=0, has_side_effects=True, vmem_limit_bytes=4 << 20),
-        )(*(pltpu.with_memory_space_constraint(x, pltpu.HBM) for x in (left_image, right_image)))
-        return pl.pallas_call(
-            scores,
-            out_shape=jax.ShapeDtypeStruct((32, 256), F32),
-            in_specs=[pl.BlockSpec(memory_space=pltpu.SMEM), VMEM],
-            out_specs=VMEM,
-            scratch_shapes=[pltpu.VMEM((256, 128), F32)],
-            name="scores",
-            compiler_params=pltpu.CompilerParams(vmem_limit_bytes=12 << 20),
-        )(ranges.T, windows)
+            compiler_params=pltpu.CompilerParams(collective_id=0, has_side_effects=True, vmem_limit_bytes=12 << 20),
+        )(ranges.T, *images)
+        return jnp.maximum(best, -2.0)
 
     return jax.shard_map(
         on_device,

time: 16.8 us -> 17.6 us (1.048)
  local copies, waits for them, and re-layouts: 0.01 us -> 0.68 us
  other arithmetic: 0 us -> 0.62 us
  Pallas kernels: 16.6 us -> 16.1 us
    unnamed x2, local copies, waits for them, and re-layouts: 0.01 us -> 0.68 us
    max x0 -> x1, other arithmetic: none -> 0.62 us  [on_device(): return jnp.maximum(best, -2.0)]
    pallas_call x2 -> x1, Pallas kernels: 16.6 us -> 16.1 us  [on_device(): pl.pallas_call(fused, out_shape=jax.ShapeDtypeStruct((32, 256), F32), in_...]
where the time goes in v2:
time: 17.6 us; the launch traced here: 17.4 us
  Pallas kernels  16.1 us (91%)
  local copies, waits for them, and re-layouts  0.68 us (4%)
  other arithmetic  0.62 us (4%)
    pallas_call x1, Pallas kernels, on_device(): pl.pallas_call(fused, out_shape=jax.ShapeDtypeStruct((32, 256), F32), in_...  16.1 us
    unnamed x2, local copies, waits for them, and re-layouts  0.68 us
    max x1, other arithmetic, on_device(): return jnp.maximum(best, -2.0)  0.62 us

profile of v2, /device:TPU:1, one launch (start us, length us, event | category | flops | bytes accessed | tf_op | source)
XLA Modules:
  0.0 17.4 jit_solution(7076367024560055732)
XLA Ops:
  0.0 0.0 copy-start
  0.0 0.7 %copy-done = s32[32,2]{0,1:T(2,128)S(1)} copy-done((s32[32,2]{0,1:T(2,128)S(1)}, s32[32,2]{0,1:T(2,128)}, u32[]{:S(2)}) %copy-start) | copy-done | bytes 280
  0.7 16.1 %exchange.1 = f32[32,256]{1,0:T(8,128)S(1)} custom-call(s32[2,32]{1,0:T(2,128)S(1)} %bitcast.1, bf16[1,8192]{1,0:T(2,128)(2,1)} %l_hbm.1, bf16[1,8192]{1,0:T(2,128)(2,1)} %r_hbm.1), custom_call_target="tpu_custom_call" | custom-call | tf_op jit(solution)/shard_map/exchange/pallas_call | solution.py:177
  16.8 0.6 %broadcast_maximum_fusion = f32[32,256]{1,0:T(8,128)} fusion(f32[32,256]{1,0:T(8,128)S(1)} %exchange.1), kind=kLoop, calls=%fused_computation | loop fusion | flops 8192 | bytes 65536 | tf_op jit(solution)/shard_map/max | solution.py:196
Async XLA Ops:
  0.0 0.7 %copy-start = (s32[32,2]{0,1:T(2,128)S(1)}, s32[32,2]{0,1:T(2,128)}, u32[]{:S(2)}) copy-start(s32[32,2]{0,1:T(2,128)} %param.5) | copy-start | bytes 772

commit v3 on v2

v3 whole, which is shorter than its diff:
```python
import jax
import jax.numpy as jnp
from jax import lax
from jax.experimental import pallas as pl
from jax.experimental.pallas import tpu as pltpu
from jax.sharding import PartitionSpec as P

F32, BF16 = jnp.float32, jnp.bfloat16
SPAN = 768
PAD = 384
MESH = pl.DeviceIdType.MESH
OFFSETS = sorted(((dy, dz) for dy in range(4) for dz in range(4)), key=lambda o: -(2 - abs(o[0] - 2)) - (2 - abs(o[1] - 2)))
PAIRS = ((0, 0), (0, 1), (1, 0), (1, 1), (0, 2), (2, 0))
TAPS = 7 * 24
DEPTH = TAPS + 8 * len(PAIRS)


def split3(x):
    hi = x.astype(BF16).astype(F32)
    mid = (x - hi).astype(BF16).astype(F32)
    return hi, mid, (x - hi) - mid


def joined(ref, tiles, *lead):
    return jnp.concatenate([ref[(*lead, pl.ds(pl.multiple_of(8 * t, 8), 8), slice(None))] for t in tiles], 0)


def kernel(rng_hbm, l_hbm, r_hbm, best_ref, rng, l_row, r_row, stage, win, lj, rj, lsum, rsum, acc, ordered,
           load_sem, own_sem, send_sem, recv_sem):
    band, tile = lax.axis_index("rows"), lax.axis_index("cols")
    bands, tiles = lax.axis_size("rows"), lax.axis_size("cols")
    width = l_hbm.shape[1]
    y, z, core = tile // 8, tile // 2 % 4, tile % 2
    goes_up = (tile < 3) & (band > 0)
    goes_down = (tile >= tiles - 3) & (band < bands - 1)
    other = jnp.where(goes_up, band - 1, band + 1)
    crosses = goes_up | goes_down
    barrier = pltpu.get_barrier_semaphore()

    loads = [pltpu.make_async_copy(a, b, load_sem.at[k])
             for k, (a, b) in enumerate(((l_hbm, l_row), (r_hbm, r_row), (rng_hbm, rng)))]
    for load in loads:
        load.start()

    def greet(other_band, other_tile):
        pl.semaphore_signal(barrier, inc=1, device_id=(other_band, other_tile), device_id_type=MESH)

    def peers(dy, dz):
        chip = (y + dy) % 4 * 8 + (z + dz) % 4 * 2
        return [chip + 1 - core] + ([chip + core] if dy or dz else [])

    @pl.when(band > 0)
    def _():
        for k in range(3):
            greet(band - 1, tiles - 3 + k)

    @pl.when(band < bands - 1)
    def _():
        for k in range(3):
            greet(band + 1, k)

    for dy, dz in OFFSETS:
        for peer in peers(dy, dz):
            greet(band, peer)

    for load in loads:
        load.wait()
    stage[:, :PAD] = jnp.zeros((2, PAD), stage.dtype)
    stage[:, PAD + width:] = jnp.zeros((2, PAD), stage.dtype)
    stage[0:1, PAD:PAD + width] = l_row[...]
    stage[1:2, PAD:PAD + width] = r_row[...]

    def window(peer):
        return stage.at[:, pl.ds(pl.multiple_of(peer * 256, 256), SPAN)]

    def send(other_band, peer, row, slot, kind):
        pltpu.make_async_remote_copy(
            src_ref=window(peer), dst_ref=win.at[row], send_sem=send_sem.at[slot], recv_sem=recv_sem.at[kind],
            device_id=(other_band, peer), device_id_type=MESH).start()

    own = pltpu.make_async_copy(window(tile), win.at[tile], own_sem)
    own.start()
    pl.semaphore_wait(barrier, tiles - 1 + jnp.where(crosses, tiles, 0))
    row_there = jnp.where(goes_up, tiles + tile, tile + 8)
    kind_there = jnp.where(goes_up, 5, 4)
    for dy, dz in OFFSETS:
        for peer in peers(dy, dz):
            send(band, peer, tile, 0, y)

        @pl.when(crosses)
        def _():
            chip = (y + dy) % 4 * 8 + (z + dz) % 4 * 2
            send(other, chip, row_there, 1, kind_there)
            send(other, chip + 1, row_there, 1, kind_there)

    def wait_for(count, sem):
        rows = win.at[pl.ds(0, count)]
        pltpu.make_async_copy(rows, rows, sem).wait()

    start = rng[0, tile]
    two = rng[1, tile] > 1

    def prepare(group, inside=None):
        w = win[pl.ds(8 * group, 8)].astype(F32)
        left, right = w[:, 0, :], w[:, 1, :]
        if inside is not None:
            left, right = jnp.where(inside, left, 0.0), jnp.where(inside, right, 0.0)
        rows = pl.ds(pl.multiple_of(8 * group, 8), 8)
        left = pltpu.roll(left, SPAN - 381, 1)
        right = pltpu.roll(right, 642 + start, 1)[:, :640]
        for ref, sums, x, cols in ((lj, lsum, left, 256), (rj, rsum, right, 512)):
            total = square = 0.0
            for j in range(7):
                v = (pltpu.roll(x, x.shape[1] - j, 1) if j else x)[:, :cols]
                ref[j, rows, :] = v
                total, square = total + v, square + v * v
            sums[0, rows, :] = total
            sums[1, rows, :] = square

    sub = lax.broadcasted_iota(jnp.int32, (8, SPAN), 0)
    halo_rows = ((sub < 3) & (band < bands - 1)) | ((sub >= 5) & (band > 0))

    def prepare_halo():
        @pl.when(band > 0)
        def _():
            wait_for(3, recv_sem.at[4])

        @pl.when(band < bands - 1)
        def _():
            wait_for(3, recv_sem.at[5])

        prepare(4, halo_rows)

    upper = lax.broadcasted_iota(jnp.int32, (128, 128), 1) >= lax.broadcasted_iota(jnp.int32, (128, 128), 0)
    lane = lax.broadcasted_iota(jnp.int32, (1, DEPTH), 1)
    place = jnp.where(lane < TAPS, lane % 24, 100 + (lane - TAPS) % 8)

    def block(step, g):
        wraps = g == 3
        trio = (g, g + 1, jnp.where(wraps, 0, g))

        def box(sums, i, cols):
            h = joined(sums, trio, i)
            near, far = h[0:8], h[8:16]
            for k in range(1, 7):
                near, far = near + h[k:k + 8], far + h[8 + k:16 + k]
            return jnp.where((sub[:, :cols] >= 5) & wraps, far, near)

        def stats(sums, cols):
            total = box(sums, 0, cols)
            mean = total * (1.0 / 49.0)
            spread = jnp.maximum(box(sums, 1, cols) * (1.0 / 49.0) - mean * mean, 0.01)
            return total, mean, lax.rsqrt(spread)

        total_l, _, scale_l = stats(lsum, 256)
        _, mean_r, scale_r = stats(rsum, 512)
        a, b = split3(-total_l), split3(mean_r)
        rt = jnp.concatenate([joined(rj, trio, j) for j in range(7)] + [b[q] for _, q in PAIRS], 0).astype(BF16)
        lt = jnp.concatenate([joined(lj, trio, j) for j in range(7)] + [a[p] for p, _ in PAIRS], 0).T.astype(BF16)
        for k in range(8):
            first = k + (jnp.where(wraps, 8, 0) if k >= 5 else 0)
            keep = ((place >= first) & (place <= first + 6)) | (place == 100 + k)
            g7 = jnp.dot(lt * keep.astype(F32).astype(BF16), rt, preferred_element_type=F32)
            for half in range(2):
                rows = slice(128 * half, 128 * half + 128)
                part = [slice(128 * (half + i), 128 * (half + i + 1)) for i in range(3)]
                s = [g7[rows, c] * scale_r[k:k + 1, c] for c in part]
                one, more = jnp.where(upper, s[1], s[2]), jnp.where(upper, s[0], s[1])
                v = jnp.where(two, jnp.maximum(one, more), one)
                acc[rows, 8 * step + k:8 * step + k + 1] = jnp.max(v, axis=1, keepdims=True)
        return scale_l * (1.0 / 49.0)

    blocks = [(y + 3 + step) % 4 for step in range(4)]
    scales = []
    own.wait()
    wait_for(7, recv_sem.at[y])
    wait_for(8, recv_sem.at[blocks[0]])
    prepare(y)
    prepare(blocks[0])
    pl.when(blocks[0] == 3)(prepare_halo)
    scales.append(block(0, blocks[0]))
    wait_for(8, recv_sem.at[blocks[2]])
    prepare(blocks[2])
    pl.when(blocks[1] == 3)(prepare_halo)
    scales.append(block(1, blocks[1]))
    wait_for(8, recv_sem.at[blocks[3]])
    prepare(blocks[3])
    pl.when((blocks[2] == 3) | (blocks[3] == 3))(prepare_halo)
    scales.append(block(2, blocks[2]))
    scales.append(block(3, blocks[3]))
    best = acc[...].T[:32]
    for step in range(4):
        ordered[pl.ds(pl.multiple_of(8 * blocks[step], 8), 8), :] = best[8 * step:8 * step + 8] * scales[step]
    best_ref[...] = pltpu.roll(ordered[...], 3, 0)

    wait_for(tiles - 1, send_sem.at[0])

    @pl.when(crosses)
    def _():
        wait_for(tiles, send_sem.at[1])


def solution(mesh):
    def on_device(left_image, right_image, ranges):
        arrays = [pltpu.with_memory_space_constraint(x, pltpu.HBM) for x in (ranges.T, left_image, right_image)]
        best = pl.pallas_call(
            kernel,
            out_shape=jax.ShapeDtypeStruct((32, 256), F32),
            in_specs=[pl.BlockSpec(memory_space=pltpu.HBM)] * 3,
            out_specs=pl.BlockSpec(memory_space=pltpu.VMEM),
            scratch_shapes=[
                pltpu.SMEM((2, 32), jnp.int32),
                pltpu.VMEM(left_image.shape, BF16),
                pltpu.VMEM(right_image.shape, BF16),
                pltpu.VMEM((2, left_image.shape[1] + 2 * PAD), BF16),
                pltpu.VMEM((40, 2, SPAN), BF16),
                pltpu.VMEM((7, 40, 256), F32),
                pltpu.VMEM((7, 40, 512), F32),
                pltpu.VMEM((2, 40, 256), F32),
                pltpu.VMEM((2, 40, 512), F32),
                pltpu.VMEM((256, 128), F32),
                pltpu.VMEM((32, 256), F32),
                pltpu.SemaphoreType.DMA((3,)),
                pltpu.SemaphoreType.DMA,
                pltpu.SemaphoreType.DMA((2,)),
                pltpu.SemaphoreType.DMA((6,)),
            ],
            name="match",
            compiler_params=pltpu.CompilerParams(collective_id=0, has_side_effects=True, vmem_limit_bytes=16 << 20),
        )(*arrays)
        return jnp.maximum(best, -2.0)

    return jax.shard_map(
        on_device,
        mesh=mesh,
        in_specs=(P(("rows", "cols"), None), P(("rows", "cols"), None), P()),
        out_specs=P("rows", "cols"),
        check_vma=False,
    )
```

time: 17.6 us -> 17.2 us (0.977)
  local copies, waits for them, and re-layouts: 0.68 us -> 0 us
  Pallas kernels: 16.1 us -> 16.4 us
    unnamed x2 -> x0, local copies, waits for them, and re-layouts: 0.68 us -> none
    pallas_call x1, Pallas kernels: 16.1 us -> 16.4 us  [on_device(): pl.pallas_call(kernel, out_shape=jax.ShapeDtypeStruct((32, 256), F32), in...]
where the time goes in v3:
time: 17.2 us; the launch traced here: 17 us
  Pallas kernels  16.4 us (95%)
  other arithmetic  0.62 us (4%)
    pallas_call x1, Pallas kernels, on_device(): pl.pallas_call(kernel, out_shape=jax.ShapeDtypeStruct((32, 256), F32), in...  16.4 us
    max x1, other arithmetic, on_device(): return jnp.maximum(best, -2.0)  0.62 us

profile of v3, /device:TPU:1, one launch (start us, length us, event | category | flops | bytes accessed | tf_op | source)
XLA Modules:
  0.0 17.0 jit_solution(9901078570441126139)
XLA Ops:
  0.0 16.4 %match.1 = f32[32,256]{1,0:T(8,128)S(1)} custom-call(s32[2,32]{1,0:T(2,128)} %bitcast.1, bf16[1,8192]{1,0:T(2,128)(2,1)} %l_hbm.1, bf16[1,8192]{1,0:T(2,128)(2,1)} %r_hbm.1), custom_call_target="tpu_custom_call" | custom-call | tf_op jit(solution)/shard_map/match/pallas_call | solution.py:206
  16.4 0.6 %broadcast_maximum_fusion = f32[32,256]{1,0:T(8,128)} fusion(f32[32,256]{1,0:T(8,128)S(1)} %match.1), kind=kLoop, calls=%fused_computation | loop fusion | flops 8192 | bytes 65536 | tf_op jit(solution)/shard_map/max | solution.py:231

commit v4 on v3

--- a/solution.py
+++ b/solution.py
@@ -11,8 +11,6 @@
 MESH = pl.DeviceIdType.MESH
 OFFSETS = sorted(((dy, dz) for dy in range(4) for dz in range(4)), key=lambda o: -(2 - abs(o[0] - 2)) - (2 - abs(o[1] - 2)))
 PAIRS = ((0, 0), (0, 1), (1, 0), (1, 1), (0, 2), (2, 0))
-TAPS = 7 * 24
-DEPTH = TAPS + 8 * len(PAIRS)
 
 
 def split3(x):
@@ -22,11 +20,11 @@
 
 
 def joined(ref, tiles, *lead):
-    return jnp.concatenate([ref[(*lead, pl.ds(pl.multiple_of(8 * t, 8), 8), slice(None))] for t in tiles], 0)
-
-
-def kernel(rng_hbm, l_hbm, r_hbm, best_ref, rng, l_row, r_row, stage, win, lj, rj, lsum, rsum, acc, ordered,
-           load_sem, own_sem, send_sem, recv_sem):
+    return jnp.concatenate([ref[(*lead, slice(8 * t, 8 * t + 8), slice(None))] for t in tiles], 0)
+
+
+def kernel(rng_hbm, l_hbm, r_hbm, best_ref, rng, l_row, r_row, stage, win, lj, rj, lsum, rsum, acc,
+           load_sem, send_sem, recv_sem):
     band, tile = lax.axis_index("rows"), lax.axis_index("cols")
     bands, tiles = lax.axis_size("rows"), lax.axis_size("cols")
     width = l_hbm.shape[1]
@@ -78,8 +76,7 @@
             src_ref=window(peer), dst_ref=win.at[row], send_sem=send_sem.at[slot], recv_sem=recv_sem.at[kind],
             device_id=(other_band, peer), device_id_type=MESH).start()
 
-    own = pltpu.make_async_copy(window(tile), win.at[tile], own_sem)
-    own.start()
+    pltpu.make_async_copy(window(tile), win.at[tile], recv_sem.at[y]).start()
     pl.semaphore_wait(barrier, tiles - 1 + jnp.where(crosses, tiles, 0))
     row_there = jnp.where(goes_up, tiles + tile, tile + 8)
     kind_there = jnp.where(goes_up, 5, 4)
@@ -101,11 +98,11 @@
     two = rng[1, tile] > 1
 
     def prepare(group, inside=None):
-        w = win[pl.ds(8 * group, 8)].astype(F32)
+        w = win[8 * group:8 * group + 8].astype(F32)
         left, right = w[:, 0, :], w[:, 1, :]
         if inside is not None:
             left, right = jnp.where(inside, left, 0.0), jnp.where(inside, right, 0.0)
-        rows = pl.ds(pl.multiple_of(8 * group, 8), 8)
+        rows = slice(8 * group, 8 * group + 8)
         left = pltpu.roll(left, SPAN - 381, 1)
         right = pltpu.roll(right, 642 + start, 1)[:, :640]
         for ref, sums, x, cols in ((lj, lsum, left, 256), (rj, rsum, right, 512)):
@@ -132,19 +129,21 @@
         prepare(4, halo_rows)
 
     upper = lax.broadcasted_iota(jnp.int32, (128, 128), 1) >= lax.broadcasted_iota(jnp.int32, (128, 128), 0)
-    lane = lax.broadcasted_iota(jnp.int32, (1, DEPTH), 1)
-    place = jnp.where(lane < TAPS, lane % 24, 100 + (lane - TAPS) % 8)
-
-    def block(step, g):
-        wraps = g == 3
-        trio = (g, g + 1, jnp.where(wraps, 0, g))
+
+    def operands(trio):
+        wraps = len(trio) == 3
 
         def box(sums, i, cols):
             h = joined(sums, trio, i)
-            near, far = h[0:8], h[8:16]
+            near = h[0:8]
             for k in range(1, 7):
-                near, far = near + h[k:k + 8], far + h[8 + k:16 + k]
-            return jnp.where((sub[:, :cols] >= 5) & wraps, far, near)
+                near = near + h[k:k + 8]
+            if not wraps:
+                return near
+            far = h[8:16]
+            for k in range(1, 7):
+                far = far + h[8 + k:16 + k]
+            return jnp.where(sub[:, :cols] >= 5, far, near)
 
         def stats(sums, cols):
             total = box(sums, 0, cols)
@@ -157,41 +156,35 @@
         a, b = split3(-total_l), split3(mean_r)
         rt = jnp.concatenate([joined(rj, trio, j) for j in range(7)] + [b[q] for _, q in PAIRS], 0).astype(BF16)
         lt = jnp.concatenate([joined(lj, trio, j) for j in range(7)] + [a[p] for p, _ in PAIRS], 0).T.astype(BF16)
+        return 8 * len(trio), lt, rt, scale_l * (1.0 / 49.0), scale_r
+
+    def block(step, taps, lt, rt, scale_l, scale_r):
+        lane = lax.broadcasted_iota(jnp.int32, (1, lt.shape[1]), 1)
+        place = jnp.where(lane < 7 * taps, lane % taps, 100 + (lane - 7 * taps) % 8)
         for k in range(8):
-            first = k + (jnp.where(wraps, 8, 0) if k >= 5 else 0)
+            first = k + (8 if taps == 24 and k >= 5 else 0)
             keep = ((place >= first) & (place <= first + 6)) | (place == 100 + k)
-            g7 = jnp.dot(lt * keep.astype(F32).astype(BF16), rt, preferred_element_type=F32)
+            g = jnp.dot(lt * keep.astype(F32).astype(BF16), rt, preferred_element_type=F32)
             for half in range(2):
                 rows = slice(128 * half, 128 * half + 128)
                 part = [slice(128 * (half + i), 128 * (half + i + 1)) for i in range(3)]
-                s = [g7[rows, c] * scale_r[k:k + 1, c] for c in part]
+                s = [g[rows, c] * scale_r[k:k + 1, c] for c in part]
                 one, more = jnp.where(upper, s[1], s[2]), jnp.where(upper, s[0], s[1])
                 v = jnp.where(two, jnp.maximum(one, more), one)
                 acc[rows, 8 * step + k:8 * step + k + 1] = jnp.max(v, axis=1, keepdims=True)
-        return scale_l * (1.0 / 49.0)
-
-    blocks = [(y + 3 + step) % 4 for step in range(4)]
-    scales = []
-    own.wait()
-    wait_for(7, recv_sem.at[y])
-    wait_for(8, recv_sem.at[blocks[0]])
-    prepare(y)
-    prepare(blocks[0])
-    pl.when(blocks[0] == 3)(prepare_halo)
-    scales.append(block(0, blocks[0]))
-    wait_for(8, recv_sem.at[blocks[2]])
-    prepare(blocks[2])
-    pl.when(blocks[1] == 3)(prepare_halo)
-    scales.append(block(1, blocks[1]))
-    wait_for(8, recv_sem.at[blocks[3]])
-    prepare(blocks[3])
-    pl.when((blocks[2] == 3) | (blocks[3] == 3))(prepare_halo)
-    scales.append(block(2, blocks[2]))
-    scales.append(block(3, blocks[3]))
-    best = acc[...].T[:32]
-    for step in range(4):
-        ordered[pl.ds(pl.multiple_of(8 * blocks[step], 8), 8), :] = best[8 * step:8 * step + 8] * scales[step]
-    best_ref[...] = pltpu.roll(ordered[...], 3, 0)
+
+    for group in range(4):
+        wait_for(8, recv_sem.at[group])
+        prepare(group)
+    parts = [operands((0, 1)), operands((1, 2)), operands((2, 3))]
+    block(0, *parts[0])
+    block(1, *parts[1])
+    prepare_halo()
+    parts.append(operands((3, 4, 0)))
+    block(2, *parts[2])
+    block(3, *parts[3])
+    best = acc[...].T[:32] * jnp.concatenate([p[3] for p in parts], 0)
+    best_ref[...] = pltpu.roll(best, 3, 0)
 
     wait_for(tiles - 1, send_sem.at[0])
 
@@ -219,9 +212,7 @@
                 pltpu.VMEM((2, 40, 256), F32),
                 pltpu.VMEM((2, 40, 512), F32),
                 pltpu.VMEM((256, 128), F32),
-                pltpu.VMEM((32, 256), F32),
                 pltpu.SemaphoreType.DMA((3,)),
-                pltpu.SemaphoreType.DMA,
                 pltpu.SemaphoreType.DMA((2,)),
                 pltpu.SemaphoreType.DMA((6,)),
             ],

time: 17.2 us -> 15.6 us (0.907)
  Pallas kernels: 16.4 us -> 14.8 us
    pallas_call x1, Pallas kernels: 16.4 us -> 14.8 us  [on_device(): pl.pallas_call(kernel, out_shape=jax.ShapeDtypeStruct((32, 256), F32), in...]
where the time goes in v4:
time: 15.6 us; the launch traced here: 15.4 us
  Pallas kernels  14.8 us (95%)
  other arithmetic  0.62 us (4%)
    pallas_call x1, Pallas kernels, on_device(): pl.pallas_call(kernel, out_shape=jax.ShapeDtypeStruct((32, 256), F32), in...  14.8 us
    max x1, other arithmetic, on_device(): return jnp.maximum(best, -2.0)  0.62 us

profile of v4, /device:TPU:1, one launch (start us, length us, event | category | flops | bytes accessed | tf_op | source)
XLA Modules:
  0.0 15.4 jit_solution(11590058935308542622)
XLA Ops:
  0.0 14.8 %match.1 = f32[32,256]{1,0:T(8,128)S(1)} custom-call(s32[2,32]{1,0:T(2,128)} %bitcast.1, bf16[1,8192]{1,0:T(2,128)(2,1)} %l_hbm.1, bf16[1,8192]{1,0:T(2,128)(2,1)} %r_hbm.1), custom_call_target="tpu_custom_call" | custom-call | tf_op jit(solution)/shard_map/match/pallas_call | solution.py:199
  14.8 0.6 %broadcast_maximum_fusion = f32[32,256]{1,0:T(8,128)} fusion(f32[32,256]{1,0:T(8,128)S(1)} %match.1), kind=kLoop, calls=%fused_computation | loop fusion | flops 8192 | bytes 65536 | tf_op jit(solution)/shard_map/max | solution.py:222

commit v5 on v4

--- a/solution.py
+++ b/solution.py
@@ -24,7 +24,7 @@
 
 
 def kernel(rng_hbm, l_hbm, r_hbm, best_ref, rng, l_row, r_row, stage, win, lj, rj, lsum, rsum, acc,
-           load_sem, send_sem, recv_sem):
+           load_sem, send_sem, recv_sem, go):
     band, tile = lax.axis_index("rows"), lax.axis_index("cols")
     bands, tiles = lax.axis_size("rows"), lax.axis_size("cols")
     width = l_hbm.shape[1]
@@ -33,12 +33,12 @@
     goes_down = (tile >= tiles - 3) & (band < bands - 1)
     other = jnp.where(goes_up, band - 1, band + 1)
     crosses = goes_up | goes_down
+    asked = ((tile < 3) & (band < bands - 1)) | ((tile >= tiles - 3) & (band > 0))
+    asker = jnp.where(tile < 3, band + 1, band - 1)
     barrier = pltpu.get_barrier_semaphore()
 
     loads = [pltpu.make_async_copy(a, b, load_sem.at[k])
              for k, (a, b) in enumerate(((l_hbm, l_row), (r_hbm, r_row), (rng_hbm, rng)))]
-    for load in loads:
-        load.start()
 
     def greet(other_band, other_tile):
         pl.semaphore_signal(barrier, inc=1, device_id=(other_band, other_tile), device_id_type=MESH)
@@ -47,20 +47,16 @@
         chip = (y + dy) % 4 * 8 + (z + dz) % 4 * 2
         return [chip + 1 - core] + ([chip + core] if dy or dz else [])
 
-    @pl.when(band > 0)
-    def _():
-        for k in range(3):
-            greet(band - 1, tiles - 3 + k)
-
-    @pl.when(band < bands - 1)
-    def _():
-        for k in range(3):
-            greet(band + 1, k)
+    @pl.when(crosses)
+    def _():
+        greet(other, tile)
 
     for dy, dz in OFFSETS:
         for peer in peers(dy, dz):
             greet(band, peer)
 
+    for load in loads:
+        load.start()
     for load in loads:
         load.wait()
     stage[:, :PAD] = jnp.zeros((2, PAD), stage.dtype)
@@ -77,15 +73,22 @@
             device_id=(other_band, peer), device_id_type=MESH).start()
 
     pltpu.make_async_copy(window(tile), win.at[tile], recv_sem.at[y]).start()
-    pl.semaphore_wait(barrier, tiles - 1 + jnp.where(crosses, tiles, 0))
+    pl.semaphore_wait(barrier, tiles - 1 + asked.astype(jnp.int32))
+
+    @pl.when(asked)
+    def _():
+        pl.semaphore_signal(go, inc=1, device_id=(asker, tile), device_id_type=MESH)
+
     row_there = jnp.where(goes_up, tiles + tile, tile + 8)
     kind_there = jnp.where(goes_up, 5, 4)
     for dy, dz in OFFSETS:
         for peer in peers(dy, dz):
             send(band, peer, tile, 0, y)
 
-        @pl.when(crosses)
-        def _():
+    @pl.when(crosses)
+    def _():
+        pl.semaphore_wait(go, 1)
+        for dy, dz in OFFSETS:
             chip = (y + dy) % 4 * 8 + (z + dz) % 4 * 2
             send(other, chip, row_there, 1, kind_there)
             send(other, chip + 1, row_there, 1, kind_there)
@@ -96,6 +99,8 @@
 
     start = rng[0, tile]
     two = rng[1, tile] > 1
+
+    within = lax.broadcasted_iota(jnp.int32, (8, 128), 1) < 2 + start
 
     def prepare(group, inside=None):
         w = win[8 * group:8 * group + 8].astype(F32)
@@ -104,7 +109,8 @@
             left, right = jnp.where(inside, left, 0.0), jnp.where(inside, right, 0.0)
         rows = slice(8 * group, 8 * group + 8)
         left = pltpu.roll(left, SPAN - 381, 1)
-        right = pltpu.roll(right, 642 + start, 1)[:, :640]
+        spun = [pltpu.roll(right[:, 128 * i:128 * i + 128], 2 + start, 1) for i in range(6)]
+        right = jnp.concatenate([jnp.where(within, a, b) for a, b in zip(spun, spun[1:])], 1)
         for ref, sums, x, cols in ((lj, lsum, left, 256), (rj, rsum, right, 512)):
             total = square = 0.0
             for j in range(7):
@@ -117,7 +123,7 @@
     sub = lax.broadcasted_iota(jnp.int32, (8, SPAN), 0)
     halo_rows = ((sub < 3) & (band < bands - 1)) | ((sub >= 5) & (band > 0))
 
-    def prepare_halo():
+    def wait_halo():
         @pl.when(band > 0)
         def _():
             wait_for(3, recv_sem.at[4])
@@ -126,7 +132,6 @@
         def _():
             wait_for(3, recv_sem.at[5])
 
-        prepare(4, halo_rows)
 
     upper = lax.broadcasted_iota(jnp.int32, (128, 128), 1) >= lax.broadcasted_iota(jnp.int32, (128, 128), 0)
 
@@ -173,14 +178,22 @@
                 v = jnp.where(two, jnp.maximum(one, more), one)
                 acc[rows, 8 * step + k:8 * step + k + 1] = jnp.max(v, axis=1, keepdims=True)
 
-    for group in range(4):
-        wait_for(8, recv_sem.at[group])
-        prepare(group)
-    parts = [operands((0, 1)), operands((1, 2)), operands((2, 3))]
+    wait_for(8, recv_sem.at[0])
+    prepare(0)
+    wait_for(8, recv_sem.at[1])
+    prepare(1)
+    wait_for(8, recv_sem.at[2])
+    prepare(2)
+    wait_for(8, recv_sem.at[3])
+    prepare(3)
+    parts = [operands((0, 1))]
+    parts.append(operands((1, 2)))
+    parts.append(operands((2, 3)))
     block(0, *parts[0])
+    wait_halo()
+    prepare(4, halo_rows)
+    parts.append(operands((3, 4, 0)))
     block(1, *parts[1])
-    prepare_halo()
-    parts.append(operands((3, 4, 0)))
     block(2, *parts[2])
     block(3, *parts[3])
     best = acc[...].T[:32] * jnp.concatenate([p[3] for p in parts], 0)
@@ -215,6 +228,7 @@
                 pltpu.SemaphoreType.DMA((3,)),
                 pltpu.SemaphoreType.DMA((2,)),
                 pltpu.SemaphoreType.DMA((6,)),
+                pltpu.SemaphoreType.REGULAR,
             ],
             name="match",
             compiler_params=pltpu.CompilerParams(collective_id=0, has_side_effects=True, vmem_limit_bytes=16 << 20),

time: 15.6 us -> 15.4 us (0.987)
  Pallas kernels: 14.8 us -> 14.6 us
where the time goes in v5:
time: 15.4 us; the launch traced here: 15.3 us
  Pallas kernels  14.6 us (95%)
  other arithmetic  0.62 us (4%)
    pallas_call x1, Pallas kernels, on_device(): pl.pallas_call(kernel, out_shape=jax.ShapeDtypeStruct((32, 256), F32), in...  14.6 us
    max x1, other arithmetic, on_device(): return jnp.maximum(best, -2.0)  0.62 us

profile of v5, /device:TPU:1, one launch (start us, length us, event | category | flops | bytes accessed | tf_op | source)
XLA Modules:
  0.0 15.3 jit_solution(5311214480687500616)
XLA Ops:
  0.0 14.6 %match.1 = f32[32,256]{1,0:T(8,128)S(1)} custom-call(s32[2,32]{1,0:T(2,128)} %bitcast.1, bf16[1,8192]{1,0:T(2,128)(2,1)} %l_hbm.1, bf16[1,8192]{1,0:T(2,128)(2,1)} %r_hbm.1), custom_call_target="tpu_custom_call" | custom-call | tf_op jit(solution)/shard_map/match/pallas_call | solution.py:212
  14.7 0.6 %broadcast_maximum_fusion = f32[32,256]{1,0:T(8,128)} fusion(f32[32,256]{1,0:T(8,128)S(1)} %match.1), kind=kLoop, calls=%fused_computation | loop fusion | flops 8192 | bytes 65536 | tf_op jit(solution)/shard_map/max | solution.py:236

commit v6 on v5

--- a/solution.py
+++ b/solution.py
@@ -23,7 +23,7 @@
     return jnp.concatenate([ref[(*lead, slice(8 * t, 8 * t + 8), slice(None))] for t in tiles], 0)
 
 
-def kernel(rng_hbm, l_hbm, r_hbm, best_ref, rng, l_row, r_row, stage, win, lj, rj, lsum, rsum, acc,
+def kernel(rng_hbm, l_hbm, r_hbm, best_ref, rng, l_row, r_row, stage, win, lj, rj, lsum, rsum, tops,
            load_sem, send_sem, recv_sem, go):
     band, tile = lax.axis_index("rows"), lax.axis_index("cols")
     bands, tiles = lax.axis_size("rows"), lax.axis_size("cols")
@@ -176,7 +176,11 @@
                 s = [g[rows, c] * scale_r[k:k + 1, c] for c in part]
                 one, more = jnp.where(upper, s[1], s[2]), jnp.where(upper, s[0], s[1])
                 v = jnp.where(two, jnp.maximum(one, more), one)
-                acc[rows, 8 * step + k:8 * step + k + 1] = jnp.max(v, axis=1, keepdims=True)
+                v = v.T
+                top = v[0:8]
+                for q in range(8, 128, 8):
+                    top = jnp.maximum(top, v[q:q + 8])
+                tops[8 * step + k, :, rows] = top
 
     wait_for(8, recv_sem.at[0])
     prepare(0)
@@ -190,13 +194,13 @@
     parts.append(operands((1, 2)))
     parts.append(operands((2, 3)))
     block(0, *parts[0])
+    block(1, *parts[1])
     wait_halo()
     prepare(4, halo_rows)
     parts.append(operands((3, 4, 0)))
-    block(1, *parts[1])
     block(2, *parts[2])
     block(3, *parts[3])
-    best = acc[...].T[:32] * jnp.concatenate([p[3] for p in parts], 0)
+    best = jnp.max(tops[...], axis=1) * jnp.concatenate([p[3] for p in parts], 0)
     best_ref[...] = pltpu.roll(best, 3, 0)
 
     wait_for(tiles - 1, send_sem.at[0])
@@ -224,7 +228,7 @@
                 pltpu.VMEM((7, 40, 512), F32),
                 pltpu.VMEM((2, 40, 256), F32),
                 pltpu.VMEM((2, 40, 512), F32),
-                pltpu.VMEM((256, 128), F32),
+                pltpu.VMEM((32, 8, 256), F32),
                 pltpu.SemaphoreType.DMA((3,)),
                 pltpu.SemaphoreType.DMA((2,)),
                 pltpu.SemaphoreType.DMA((6,)),

time: 15.4 us -> 15.4 us (level)
  no operation moved by 1% of the time
where the time goes in v6:
time: 15.4 us; the launch traced here: 15.2 us
  Pallas kernels  14.6 us (95%)
  other arithmetic  0.62 us (4%)
    pallas_call x1, Pallas kernels, on_device(): pl.pallas_call(kernel, out_shape=jax.ShapeDtypeStruct((32, 256), F32), in...  14.6 us
    max x1, other arithmetic, on_device(): return jnp.maximum(best, -2.0)  0.62 us

profile of v6, /device:TPU:1, one launch (start us, length us, event | category | flops | bytes accessed | tf_op | source)
XLA Modules:
  0.0 15.2 jit_solution(8021542060863882902)
XLA Ops:
  0.0 14.6 %match.1 = f32[32,256]{1,0:T(8,128)S(1)} custom-call(s32[2,32]{1,0:T(2,128)} %bitcast.1, bf16[1,8192]{1,0:T(2,128)(2,1)} %l_hbm.1, bf16[1,8192]{1,0:T(2,128)(2,1)} %r_hbm.1), custom_call_target="tpu_custom_call" | custom-call | tf_op jit(solution)/shard_map/match/pallas_call | solution.py:216
  14.6 0.6 %broadcast_maximum_fusion = f32[32,256]{1,0:T(8,128)} fusion(f32[32,256]{1,0:T(8,128)S(1)} %match.1), kind=kLoop, calls=%fused_computation | loop fusion | flops 8192 | bytes 65536 | tf_op jit(solution)/shard_map/max | solution.py:240

commit v7 on v6

--- a/solution.py
+++ b/solution.py
@@ -187,8 +187,8 @@
     wait_for(8, recv_sem.at[1])
     prepare(1)
     wait_for(8, recv_sem.at[2])
+    wait_for(8, recv_sem.at[3])
     prepare(2)
-    wait_for(8, recv_sem.at[3])
     prepare(3)
     parts = [operands((0, 1))]
     parts.append(operands((1, 2)))

time: 15.4 us -> 15.2 us (0.987)
  Pallas kernels: 14.6 us -> 14.4 us
where the time goes in v7:
time: 15.2 us; the launch traced here: 15.1 us
  Pallas kernels  14.4 us (95%)
  other arithmetic  0.62 us (4%)
    pallas_call x1, Pallas kernels, on_device(): pl.pallas_call(kernel, out_shape=jax.ShapeDtypeStruct((32, 256), F32), in...  14.4 us
    max x1, other arithmetic, on_device(): return jnp.maximum(best, -2.0)  0.62 us

profile of v7, /device:TPU:1, one launch (start us, length us, event | category | flops | bytes accessed | tf_op | source)
XLA Modules:
  0.0 15.1 jit_solution(16602487356794636857)
XLA Ops:
  0.0 14.4 %match.1 = f32[32,256]{1,0:T(8,128)S(1)} custom-call(s32[2,32]{1,0:T(2,128)} %bitcast.1, bf16[1,8192]{1,0:T(2,128)(2,1)} %l_hbm.1, bf16[1,8192]{1,0:T(2,128)(2,1)} %r_hbm.1), custom_call_target="tpu_custom_call" | custom-call | tf_op jit(solution)/shard_map/match/pallas_call | solution.py:216
  14.4 0.6 %broadcast_maximum_fusion = f32[32,256]{1,0:T(8,128)} fusion(f32[32,256]{1,0:T(8,128)S(1)} %match.1), kind=kLoop, calls=%fused_computation | loop fusion | flops 8192 | bytes 65536 | tf_op jit(solution)/shard_map/max | solution.py:240

commit v8 on v7

--- a/solution.py
+++ b/solution.py
@@ -6,8 +6,8 @@
 from jax.sharding import PartitionSpec as P
 
 F32, BF16 = jnp.float32, jnp.bfloat16
-SPAN = 768
-PAD = 384
+SPAN = 640
+PAD = 381
 MESH = pl.DeviceIdType.MESH
 OFFSETS = sorted(((dy, dz) for dy in range(4) for dz in range(4)), key=lambda o: -(2 - abs(o[0] - 2)) - (2 - abs(o[1] - 2)))
 PAIRS = ((0, 0), (0, 1), (1, 0), (1, 1), (0, 2), (2, 0))
@@ -59,8 +59,8 @@
         load.start()
     for load in loads:
         load.wait()
-    stage[:, :PAD] = jnp.zeros((2, PAD), stage.dtype)
-    stage[:, PAD + width:] = jnp.zeros((2, PAD), stage.dtype)
+    stage[:, :384] = jnp.zeros((2, 384), stage.dtype)
+    stage[:, width + 256:] = jnp.zeros((2, 128), stage.dtype)
     stage[0:1, PAD:PAD + width] = l_row[...]
     stage[1:2, PAD:PAD + width] = r_row[...]
 
@@ -100,7 +100,7 @@
     start = rng[0, tile]
     two = rng[1, tile] > 1
 
-    within = lax.broadcasted_iota(jnp.int32, (8, 128), 1) < 2 + start
+    within = lax.broadcasted_iota(jnp.int32, (8, 128), 1) < 5 + start
 
     def prepare(group, inside=None):
         w = win[8 * group:8 * group + 8].astype(F32)
@@ -108,9 +108,9 @@
         if inside is not None:
             left, right = jnp.where(inside, left, 0.0), jnp.where(inside, right, 0.0)
         rows = slice(8 * group, 8 * group + 8)
-        left = pltpu.roll(left, SPAN - 381, 1)
-        spun = [pltpu.roll(right[:, 128 * i:128 * i + 128], 2 + start, 1) for i in range(6)]
-        right = jnp.concatenate([jnp.where(within, a, b) for a, b in zip(spun, spun[1:])], 1)
+        left = pltpu.roll(left[:, 256:], 384 - 122, 1)
+        spun = [pltpu.roll(right[:, 128 * i:128 * i + 128], 5 + start, 1) for i in range(5)]
+        right = jnp.concatenate([jnp.where(within, a, b) for a, b in zip(spun, spun[1:] + spun[:1])], 1)
         for ref, sums, x, cols in ((lj, lsum, left, 256), (rj, rsum, right, 512)):
             total = square = 0.0
             for j in range(7):
@@ -222,7 +222,7 @@
                 pltpu.SMEM((2, 32), jnp.int32),
                 pltpu.VMEM(left_image.shape, BF16),
                 pltpu.VMEM(right_image.shape, BF16),
-                pltpu.VMEM((2, left_image.shape[1] + 2 * PAD), BF16),
+                pltpu.VMEM((2, left_image.shape[1] + 384), BF16),
                 pltpu.VMEM((40, 2, SPAN), BF16),
                 pltpu.VMEM((7, 40, 256), F32),
                 pltpu.VMEM((7, 40, 512), F32),

time: 15.2 us -> 15.2 us (level)
  no operation moved by 1% of the time
where the time goes in v8:
time: 15.2 us; the launch traced here: 15.1 us
  Pallas kernels  14.4 us (95%)
  other arithmetic  0.62 us (4%)
    pallas_call x1, Pallas kernels, on_device(): pl.pallas_call(kernel, out_shape=jax.ShapeDtypeStruct((32, 256), F32), in...  14.4 us
    max x1, other arithmetic, on_device(): return jnp.maximum(best, -2.0)  0.62 us

profile of v8, /device:TPU:1, one launch (start us, length us, event | category | flops | bytes accessed | tf_op | source)
XLA Modules:
  0.0 15.1 jit_solution(8641936421285155527)
XLA Ops:
  0.0 14.4 %match.1 = f32[32,256]{1,0:T(8,128)S(1)} custom-call(s32[2,32]{1,0:T(2,128)} %bitcast.1, bf16[1,8192]{1,0:T(2,128)(2,1)} %l_hbm.1, bf16[1,8192]{1,0:T(2,128)(2,1)} %r_hbm.1), custom_call_target="tpu_custom_call" | custom-call | tf_op jit(solution)/shard_map/match/pallas_call | solution.py:216
  14.4 0.6 %broadcast_maximum_fusion = f32[32,256]{1,0:T(8,128)} fusion(f32[32,256]{1,0:T(8,128)S(1)} %match.1), kind=kLoop, calls=%fused_computation | loop fusion | flops 8192 | bytes 65536 | tf_op jit(solution)/shard_map/max | solution.py:240

commit v9 on v7

--- a/solution.py
+++ b/solution.py
@@ -108,7 +108,7 @@
         if inside is not None:
             left, right = jnp.where(inside, left, 0.0), jnp.where(inside, right, 0.0)
         rows = slice(8 * group, 8 * group + 8)
-        left = pltpu.roll(left, SPAN - 381, 1)
+        left = pltpu.roll(left[:, 256:], 512 - 125, 1)[:, :384]
         spun = [pltpu.roll(right[:, 128 * i:128 * i + 128], 2 + start, 1) for i in range(6)]
         right = jnp.concatenate([jnp.where(within, a, b) for a, b in zip(spun, spun[1:])], 1)
         for ref, sums, x, cols in ((lj, lsum, left, 256), (rj, rsum, right, 512)):

time: 15.2 us -> 15.2 us (level)
  no operation moved by 1% of the time
where the time goes in v9:
time: 15.2 us; the launch traced here: 15.1 us
  Pallas kernels  14.4 us (95%)
  other arithmetic  0.62 us (4%)
    pallas_call x1, Pallas kernels, on_device(): pl.pallas_call(kernel, out_shape=jax.ShapeDtypeStruct((32, 256), F32), in...  14.4 us
    max x1, other arithmetic, on_device(): return jnp.maximum(best, -2.0)  0.62 us

profile of v9, /device:TPU:1, one launch (start us, length us, event | category | flops | bytes accessed | tf_op | source)
XLA Modules:
  0.0 15.1 jit_solution(16602487356794636857)
XLA Ops:
  0.0 14.4 %match.1 = f32[32,256]{1,0:T(8,128)S(1)} custom-call(s32[2,32]{1,0:T(2,128)} %bitcast.1, bf16[1,8192]{1,0:T(2,128)(2,1)} %l_hbm.1, bf16[1,8192]{1,0:T(2,128)(2,1)} %r_hbm.1), custom_call_target="tpu_custom_call" | custom-call | tf_op jit(solution)/shard_map/match/pallas_call | solution.py:216
  14.4 0.6 %broadcast_maximum_fusion = f32[32,256]{1,0:T(8,128)} fusion(f32[32,256]{1,0:T(8,128)S(1)} %match.1), kind=kLoop, calls=%fused_computation | loop fusion | flops 8192 | bytes 65536 | tf_op jit(solution)/shard_map/max | solution.py:240

commit v10 on v9

--- a/solution.py
+++ b/solution.py
@@ -133,6 +133,7 @@
             wait_for(3, recv_sem.at[5])
 
 
+    inner = (lax.broadcasted_iota(jnp.int32, (128, 128), 1) + jnp.where(two, 128, 0)) >= lax.broadcasted_iota(jnp.int32, (128, 128), 0)
     upper = lax.broadcasted_iota(jnp.int32, (128, 128), 1) >= lax.broadcasted_iota(jnp.int32, (128, 128), 0)
 
     def operands(trio):
@@ -174,8 +175,7 @@
                 rows = slice(128 * half, 128 * half + 128)
                 part = [slice(128 * (half + i), 128 * (half + i + 1)) for i in range(3)]
                 s = [g[rows, c] * scale_r[k:k + 1, c] for c in part]
-                one, more = jnp.where(upper, s[1], s[2]), jnp.where(upper, s[0], s[1])
-                v = jnp.where(two, jnp.maximum(one, more), one)
+                v = jnp.maximum(jnp.where(inner, s[1], s[2]), jnp.where(upper, jnp.where(two, s[0], s[1]), s[2]))
                 v = v.T
                 top = v[0:8]
                 for q in range(8, 128, 8):

time: 15.2 us -> 15.3 us (level)
  no operation moved by 1% of the time
where the time goes in v10:
time: 15.3 us; the launch traced here: 15.1 us
  Pallas kernels  14.5 us (95%)
  other arithmetic  0.62 us (4%)
    pallas_call x1, Pallas kernels, on_device(): pl.pallas_call(kernel, out_shape=jax.ShapeDtypeStruct((32, 256), F32), in...  14.5 us
    max x1, other arithmetic, on_device(): return jnp.maximum(best, -2.0)  0.62 us

profile of v10, /device:TPU:1, one launch (start us, length us, event | category | flops | bytes accessed | tf_op | source)
XLA Modules:
  0.0 15.1 jit_solution(3610631826078070536)
XLA Ops:
  0.0 14.5 %match.1 = f32[32,256]{1,0:T(8,128)S(1)} custom-call(s32[2,32]{1,0:T(2,128)} %bitcast.1, bf16[1,8192]{1,0:T(2,128)(2,1)} %l_hbm.1, bf16[1,8192]{1,0:T(2,128)(2,1)} %r_hbm.1), custom_call_target="tpu_custom_call" | custom-call | tf_op jit(solution)/shard_map/match/pallas_call | solution.py:216
  14.5 0.6 %broadcast_maximum_fusion = f32[32,256]{1,0:T(8,128)} fusion(f32[32,256]{1,0:T(8,128)S(1)} %match.1), kind=kLoop, calls=%fused_computation | loop fusion | flops 8192 | bytes 65536 | tf_op jit(solution)/shard_map/max | solution.py:240
